TPU v7x, 256 devices: a whole 4x4x8 slice. The times are simulated.
256 devices in a mesh: pts: 64 (over z, x, core), blk: 4 (over y).
Axes of the slice: x: 4, y: 4, z: 8, core: 2. Of those that a mesh axis runs over, the one named last changes fastest.
Arguments:
- points: bfloat16 [2097152, 128], P(('pts', 'blk')), may hold values from -1.5 to 1.5
- targets: float32 [2097152, 64], P(('pts', 'blk')), may hold values from -6 to 6
- coefs: float32 [2097152, 64], P(('pts', 'blk')), may hold values from -0.5 to 0.5
- preds: float32 [2097152, 64], P(('pts', 'blk')), may hold values from -32 to 32
- block_inverse: float32 [2048, 2048], P('blk'), may hold values from -0.2 to 2.2
- block_id: int32 [1], replicated, may hold values from 0 to 1023
Outputs:
- new_coefs: float32 [2097152, 64], P(('pts', 'blk'))
- new_preds: float32 [2097152, 64], P(('pts', 'blk'))
All inputs are finite; a program needn't handle non-finite values.
Results may differ from a plain program's by a relative error of at most 0.0042.
Values may be sent and summed in bfloat16 or wider, within the bound.
A program may use at most 128 MiB of HBM per device.

v0:
```python
import jax
import jax.numpy as jnp
from jax import lax
from jax.sharding import Mesh
from jax.sharding import PartitionSpec as P

PTS_BLK = ("pts_0", "pts_1", "pts_2", "blk")
damping = 1.0
inverse_width = 0.25


def spread(value, axes, root):
    value = jnp.where(lax.axis_index(axes) == root, value, jnp.zeros_like(value))
    for axis in axes:
        value = lax.psum(value, axis)
    return value


def in_blocks(value, dim, length):
    before, after = (value.shape[:dim], value.shape[dim + 1 :])
    return jnp.moveaxis(value.reshape(*before, length, -1, *after), dim, 0)


def sum_at_owner(value, axis, dim):
    pieces = in_blocks(value, dim, lax.axis_size(axis))
    arrived = lax.all_to_all(pieces, axis, split_axis=0, concat_axis=0, tiled=True)
    return arrived.sum(axis=0)


def summed_rows(value, axes, dim):
    far, near = axes
    pieces = in_blocks(value, dim, lax.axis_size(far))
    nearer = sum_at_owner(pieces, near, dim + 1)
    arrived = lax.all_to_all(nearer, far, split_axis=0, concat_axis=0, tiled=True)
    return arrived.sum(axis=0)


def filled_up(lines, length):
    spare = -len(lines) % length
    return jnp.pad(lines, [(0, spare)] + [(0, 0)] * (lines.ndim - 1))


def from_everyone(value, axis):
    copies = jnp.broadcast_to(value, (lax.axis_size(axis), *value.shape))
    return lax.all_to_all(copies, axis, split_axis=0, concat_axis=0, tiled=True)


def laid_out(pieces, dim):
    pieces = jnp.moveaxis(pieces, 0, dim)
    lengths = pieces.shape
    return pieces.reshape(*lengths[:dim], lengths[dim] * lengths[dim + 1], *lengths[dim + 2 :])


def gather_axes(value, axes, dim):
    far, near = axes
    pieces = from_everyone(from_everyone(value, far), near)
    return laid_out(pieces.swapaxes(0, 1).reshape(-1, *value.shape), dim)


def total_of(value, axes):
    lines = value.reshape(-1, value.shape[-1])
    own = summed_rows(filled_up(lines, lax.axis_size(axes[0]) * lax.axis_size(axes[1])), axes, 0)
    whole = gather_axes(own, axes, 0)
    return whole[: len(lines)].reshape(value.shape)


def gathered_copies(value, axis, dim):
    return laid_out(from_everyone(value, axis), dim)


def kernel_rows(centers, others):
    center_wide = centers.astype(jnp.float32)
    other_wide = others.astype(jnp.float32)
    center_squares = jnp.sum(center_wide * center_wide, axis=1)
    point_squares = jnp.sum(other_wide * other_wide, axis=1)
    inner_products = jnp.dot(centers, others.T, preferred_element_type=jnp.float32)
    distance = center_squares[:, None] + point_squares[None, :] - 2.0 * inner_products
    return jnp.exp(-inverse_width * distance).astype(jnp.bfloat16)


def body(points, targets, coefs, preds, block_inverse, block_id):
    shard_rows = points.shape[0]
    block_order = block_inverse.shape[1]
    targets_width = targets.shape[1]
    block_start = block_id[0] * block_order
    owner_index = block_start // shard_rows
    offset = block_start % shard_rows
    is_owner = lax.axis_index(PTS_BLK) == owner_index
    local_centers = lax.dynamic_slice_in_dim(points, offset, block_order, 0)
    centers = spread(local_centers, PTS_BLK, owner_index)
    tile_width = min(512, shard_rows)
    tile_count = shard_rows // tile_width
    point_tiles = points.reshape(tile_count, tile_width, points.shape[1])
    coef_tiles = coefs.astype(jnp.bfloat16).reshape(tile_count, tile_width, targets_width)
    kernel = lax.map(lambda tile_points: kernel_rows(centers, tile_points), point_tiles)
    summed = jnp.einsum("nbs,nsd->bd", kernel, coef_tiles, preferred_element_type=jnp.float32)
    block_coefs = lax.dynamic_slice_in_dim(coefs, offset, block_order, 0)
    own_block = lax.dynamic_slice_in_dim(targets, offset, block_order, 0) - damping * block_coefs
    own_term = jnp.where(is_owner, own_block, 0.0) - summed
    slab_part = sum_at_owner(own_term, "blk", 0)
    slab_part = total_of(slab_part, (("pts_0", "pts_1"), "pts_2"))
    residual = gathered_copies(slab_part, "blk", 0)
    slab_update = jnp.dot(block_inverse, residual, precision=lax.Precision.HIGHEST)
    update = gathered_copies(slab_update, "blk", 0)
    new_coefs = jnp.where(
        is_owner, lax.dynamic_update_slice_in_dim(coefs, block_coefs + update, offset, 0), coefs
    )
    update_half = update.astype(jnp.bfloat16)
    shifts = jnp.einsum("nbs,bd->nsd", kernel, update_half, preferred_element_type=jnp.float32)
    new_preds = preds + shifts.reshape(shard_rows, targets_width)
    return (new_coefs, new_preds)


def solution(mesh):
    split = Mesh(
        mesh.devices.reshape(8, 4, 2, mesh.shape["blk"]), ("pts_0", "pts_1", "pts_2", "blk")
    )
    in_specs = (
        P(PTS_BLK, None),
        P(PTS_BLK, None),
        P(PTS_BLK, None),
        P(PTS_BLK, None),
        P("blk", None),
        P(),
    )
    out_specs = (P(PTS_BLK, None), P(PTS_BLK, None))
    return jax.shard_map(body, mesh=split, in_specs=in_specs, out_specs=out_specs, check_vma=False)
```

profile of v0, /device:TPU:1, one launch (start us, length us, event | category | flops | bytes accessed | tf_op | source)
XLA Modules:
  0.0 446.5 jit_solution(14518260487018970397)
XLA Ops:
  7.2 1.6 copy.69
  9.5 2.0 dynamic-slice_select_fusion
  11.6 73.0 %all-reduce.5.cloned.1.call-done = bf16[2048,128]{1,0:T(8,128)(2,1)} async-done(((bf16[2048,128]{1,0:T(8,128)(2,1)}), bf16[2048,128]{1,0:T(8,128)(2,1)}) %all-reduce.5.cloned.1.call-update) | async-done | bytes 524304 | tf_op jit(solution)/shard_map/psum | solution.py:15
  84.6 51.3 %all-reduce.7.cloned.1.call-done = bf16[2048,128]{1,0:T(8,128)(2,1)} async-done(((bf16[2048,128]{1,0:T(8,128)(2,1)}), bf16[2048,128]{1,0:T(8,128)(2,1)}) %all-reduce.7.cloned.1.call-update) | async-done | bytes 524304 | tf_op jit(solution)/shard_map/psum | solution.py:15
  136.0 35.4 %all-reduce.9.cloned.1.call-done = bf16[2048,128]{1,0:T(8,128)(2,1)} async-done(((bf16[2048,128]{1,0:T(8,128)(2,1)}), bf16[2048,128]{1,0:T(8,128)(2,1)}) %all-reduce.9.cloned.1.call-update) | async-done | bytes 524304 | tf_op jit(solution)/shard_map/psum | solution.py:15
  171.6 48.7 %all-reduce.11.cloned.1.call-done = bf16[2048,128]{1,0:T(8,128)(2,1)} async-done(((bf16[2048,128]{1,0:T(8,128)(2,1)}), bf16[2048,128]{1,0:T(8,128)(2,1)}) %all-reduce.11.cloned.1.call-update) | async-done | bytes 524304 | tf_op jit(solution)/shard_map/psum | solution.py:15
  220.3 96.1 %while.10 = (s32[]{:T(128)}, bf16[16,2048,512]{1,2,0:T(8,128)(2,1)}, bf16[2048,128]{1,0:T(8,128)(2,1)}, bf16[16,512,128]{2,1,0:T(8,128)(2,1)}, s32[]{:T(128)}) while((s32[]{:T(128)}, bf16[16,2048,512]{1,2,0:T(8,128)(2,1)}, bf16[2048,128]{1,0:T(8,128)(2,1)}, bf16[16,512,128]{2,1,0:T(8,128)(2,1)}, s32[]{:T(128)}) %tuple.33), condition=%wide.region_7.8_spmd, body=%wide.region_4.7_spmd.sunk | while | flops 274658816 | bytes 3429441 | solution.py:95
  220.3 1.0 multiply_reduce_fusion.4
  221.3 1.4 multiply_reduce_fusion.5
  222.7 3.6 fusion.22
  226.3 1.0 multiply_reduce_fusion.4
  227.4 1.4 multiply_reduce_fusion.5
  228.8 3.5 fusion.22
  232.3 1.0 multiply_reduce_fusion.4
  233.3 1.4 multiply_reduce_fusion.5
  234.7 3.6 fusion.22
  238.3 1.0 multiply_reduce_fusion.4
  239.3 1.4 multiply_reduce_fusion.5
  240.7 3.6 fusion.22
  244.3 1.0 multiply_reduce_fusion.4
  245.3 1.4 multiply_reduce_fusion.5
  246.7 3.6 fusion.22
  250.3 1.0 multiply_reduce_fusion.4
  251.4 1.4 multiply_reduce_fusion.5
  252.8 3.5 fusion.22
  256.3 1.0 multiply_reduce_fusion.4
  257.4 1.4 multiply_reduce_fusion.5
  258.8 3.6 fusion.22
  262.3 1.0 multiply_reduce_fusion.4
  263.4 1.4 multiply_reduce_fusion.5
  264.8 3.6 fusion.22
  268.3 1.0 multiply_reduce_fusion.4
  269.4 1.4 multiply_reduce_fusion.5
  270.8 3.6 fusion.22
  274.4 1.0 multiply_reduce_fusion.4
  275.4 1.4 multiply_reduce_fusion.5
  276.8 3.5 fusion.22
  280.3 1.0 multiply_reduce_fusion.4
  281.4 1.4 multiply_reduce_fusion.5
  282.8 3.5 fusion.22
  286.3 1.0 multiply_reduce_fusion.4
  287.4 1.4 multiply_reduce_fusion.5
  288.8 3.6 fusion.22
  293.4 1.4 multiply_reduce_fusion.5
  294.8 3.6 fusion.22
  298.4 1.0 multiply_reduce_fusion.4
  299.4 1.4 multiply_reduce_fusion.5
  300.8 3.5 fusion.22
  304.3 1.0 multiply_reduce_fusion.4
  305.4 1.4 multiply_reduce_fusion.5
  306.8 3.6 fusion.22
  310.4 1.0 multiply_reduce_fusion.4
  311.4 1.4 multiply_reduce_fusion.5
  312.8 3.5 fusion.22
  316.3 14.1 %fusion.8 = f32[2048,64]{0,1:T(8,128)S(1)} fusion(bf16[16,2048,512]{1,2,0:T(8,128)(2,1)} %get-tuple-element.24, bf16[8,16,8,512]{3,2,1,0:T(8,128)(2,1)S(1)} %bitcast.68, f32[8192,64]{0,1:T(8,128)} %param.9, s32[]{:T(128)S(6)} %select_n.44, f32[8192,64]{0,1:T(8,128)S(1)} %copy.69, pred[]{:T(512)S(6)} %eq.6), kind=kOutput, calls=%fused_computation.13 | convolution fusion | flops 2147876864 | bytes 36175876 | tf_op jit(solution)/shard_map/nbs,nsd->bd/dot_general | solution.py:96
  330.5 10.2 %all_to_all.35 = f32[4,512,64]{1,2,0:T(8,128)S(1)} all-to-all(f32[4,512,64]{1,2,0:T(8,128)S(1)} %bitcast.72), channel_id=1, replica_groups=mesh['pts_0'=8,'pts_1'=4,'pts_2'=2,'blk'=4] {'blk'}, dimensions={0} | all-to-all | bytes 1048576 | tf_op jit(solution)/shard_map/all_to_all | solution.py:26
  341.1 7.7 %all_to_all.36 = f32[2,1,16384]{2,1,0:T(1,128)S(1)} all-to-all(f32[2,1,16384]{2,1,0:T(1,128)S(1)} %reshape.32), channel_id=1, replica_groups=mesh['pts_0'=8,'pts_1'=4,'pts_2'=2,'blk'=4] {'pts_2'}, dimensions={0} | all-to-all | bytes 262144 | tf_op jit(solution)/shard_map/all_to_all | solution.py:26
  350.7 18.1 %all_to_all.37 = f32[32,1,512]{2,1,0:T(1,128)S(1)} all-to-all(f32[32,1,512]{2,1,0:T(1,128)S(1)} %reshape.34), channel_id=1, replica_groups=mesh['pts_0'=8,'pts_1'=4,'pts_2'=2,'blk'=4] {'pts_0','pts_1'}, dimensions={0} | all-to-all | bytes 131072 | tf_op jit(solution)/shard_map/all_to_all | solution.py:34
  369.9 12.0 %all_to_all.38 = f32[32,1,512]{2,1,0:T(1,128)S(1)} all-to-all(f32[32,1,512]{2,1,0:T(1,128)S(1)} %reshape.36), channel_id=1, replica_groups=mesh['pts_0'=8,'pts_1'=4,'pts_2'=2,'blk'=4] {'pts_0','pts_1'}, dimensions={0} | all-to-all | bytes 131072 | tf_op jit(solution)/shard_map/all_to_all | solution.py:45
  383.0 6.4 %all_to_all.39 = f32[2,1,16384]{2,1,0:T(1,128)S(1)} all-to-all(f32[2,1,16384]{2,1,0:T(1,128)S(1)} %reshape.38), channel_id=1, replica_groups=mesh['pts_0'=8,'pts_1'=4,'pts_2'=2,'blk'=4] {'pts_2'}, dimensions={0} | all-to-all | bytes 262144 | tf_op jit(solution)/shard_map/all_to_all | solution.py:45
  390.8 11.6 %all_to_all.40 = f32[4,512,64]{1,2,0:T(8,128)S(1)} all-to-all(f32[4,512,64]{1,2,0:T(8,128)S(1)} %broadcast_in_dim.33), channel_id=1, replica_groups=mesh['pts_0'=8,'pts_1'=4,'pts_2'=2,'blk'=4] {'blk'}, dimensions={0} | all-to-all | bytes 1048576 | tf_op jit(solution)/shard_map/all_to_all | solution.py:45
  402.5 6.3 %convolution_bitcast_fusion.1 = f32[512,64]{0,1:T(8,128)S(1)} fusion(f32[2048,64]{0,1:T(8,128)S(1)} %bitcast.71, f32[512,2048]{1,0:T(8,128)} %param.12), kind=kOutput, calls=%fused_computation.14 | convolution fusion | flops 805306368 | bytes 4849664 | tf_op jit(solution)/shard_map/dot_general | solution.py:103
  408.8 10.9 %all_to_all.41 = f32[4,512,64]{1,2,0:T(8,128)S(1)} all-to-all(f32[4,512,64]{1,2,0:T(8,128)S(1)} %broadcast_in_dim.34), channel_id=1, replica_groups=mesh['pts_0'=8,'pts_1'=4,'pts_2'=2,'blk'=4] {'blk'}, dimensions={0} | all-to-all | bytes 1048576 | tf_op jit(solution)/shard_map/all_to_all | solution.py:45
  421.0 19.1 %convolution_add_fusion = f32[8192,64]{0,1:T(8,128)} fusion(f32[8192,64]{0,1:T(8,128)} %param.11, bf16[8192,2048]{1,0:T(8,128)(2,1)} %bitcast.67, bf16[2048,64]{0,1:T(8,128)(2,1)S(1)} %bitcast.75), kind=kOutput, calls=%fused_computation.11 | convolution fusion | flops 2148007936 | bytes 38010880 | tf_op jit(solution)/shard_map/nbs,bd->nsd/dot_general | solution.py:109
  (44 shorter events, 8.4 us)
Async XLA Ops:
  7.2 77.4 %all-reduce.5.cloned.1.call-start = ((), (), s32[]{:S(2)}) async-start(), calls=%async_computation.7 | async-start | bytes 1048576 | tf_op jit(solution)/shard_map/psum | solution.py:15
  11.5 124.4 %all-reduce.7.cloned.1.call-start = ((), (), s32[]{:S(2)}) async-start(), calls=%async_computation.8 | async-start | bytes 1048576 | tf_op jit(solution)/shard_map/psum | solution.py:15
  84.6 86.9 %all-reduce.9.cloned.1.call-start = ((), (), s32[]{:S(2)}) async-start(), calls=%async_computation.9 | async-start | bytes 1048576 | tf_op jit(solution)/shard_map/psum | solution.py:15
  136.0 84.3 %all-reduce.11.cloned.1.call-start = ((), (), s32[]{:S(2)}) async-start(), calls=%async_computation.10 | async-start | bytes 1048576 | tf_op jit(solution)/shard_map/psum | solution.py:15
  420.9 19.1 %copy-start = (f32[8192,64]{0,1:T(8,128)}, f32[8192,64]{0,1:T(8,128)S(1)}, u32[]{:S(2)}) copy-start(f32[8192,64]{0,1:T(8,128)S(1)} %select_n.49) | copy-start | bytes 6291460
Sparse Core Ops, SparseCore 0:
  11.7 72.8 all-reduce.4
  86.9 49.0 all-reduce.6
  138.6 32.8 all-reduce.8
  173.6 46.5 all-reduce.10
where the time goes:
time: 448 us; the launch traced here: 447 us
  waiting for transfers between devices  208 us (46%)
  matrix products  96.4 us (22%)
  blocking collectives  77 us (17%)
  other arithmetic  45.1 us (10%)
  between operations  14.7 us (3%)
  local copies, waits for them, and re-layouts  4.66 us (1%)
    psum x4, waiting for transfers between devices, spread(): value = lax.psum(value, axis)  208 us
    dot_general x16, matrix products, kernel_rows(): jnp.dot(centers, others.T, preferred_element_type=jnp.float32)  56.9 us
    all_to_all x4, blocking collectives, from_everyone(): return lax.all_to_all(copies, axis, split_axis=0, concat_axis=0, tiled=True)  41 us
    reduce_sum x16, other arithmetic, kernel_rows(): center_squares = jnp.sum(center_wide * center_wide, axis=1)  22.2 us
    dot_general x1, matrix products, body(): jnp.einsum('nbs,bd->nsd', kernel, update_half, preferred_element_type=jnp...  19.1 us
    all_to_all x1, blocking collectives, summed_rows(): lax.all_to_all(nearer, far, split_axis=0, concat_axis=0, tiled=True)  18.1 us
    all_to_all x2, blocking collectives, sum_at_owner(): lax.all_to_all(pieces, axis, split_axis=0, concat_axis=0, tiled=True)  17.9 us
    reduce_sum x16, other arithmetic, kernel_rows(): point_squares = jnp.sum(other_wide * other_wide, axis=1)  16.8 us
  transfers between devices with their start and end apart: 4, of which 4 were waited for; matrix products, arithmetic and copies ran while one was open for 0% of the time, Pallas kernels for 0%

commit v1 on v0

--- a/solution.py
+++ b/solution.py
@@ -12,7 +12,7 @@
 def spread(value, axes, root):
     value = jnp.where(lax.axis_index(axes) == root, value, jnp.zeros_like(value))
     for axis in axes:
-        value = lax.psum(value, axis)
+        value = lax.all_gather(value, axis).sum(axis=0)
     return value
 
 

time: 448 us -> 371 us (0.83)
  waiting for transfers between devices: 208 us -> 139 us
  other arithmetic: 45.1 us -> 40.4 us
    psum x4 -> x0, waiting for transfers between devices: 208 us -> none  [spread(): value = lax.psum(value, axis)]
    all_gather x0 -> x4, waiting for transfers between devices: none -> 139 us  [spread(): value = lax.all_gather(value, axis).sum(axis=0)]
    reduce_sum x16, other arithmetic: 22.2 us -> 5.5 us  [kernel_rows(): center_squares = jnp.sum(center_wide * center_wide, axis=1)]
    reduce_sum x0 -> x4, other arithmetic: none -> 11.1 us  [spread(): value = lax.all_gather(value, axis).sum(axis=0)]
where the time goes in v1:
time: 371 us; the launch traced here: 370 us
  waiting for transfers between devices  139 us (37%)
  matrix products  95.6 us (26%)
  blocking collectives  75.6 us (20%)
  other arithmetic  40.4 us (11%)
  between operations  14.7 us (4%)
  local copies, waits for them, and re-layouts  4.66 us (1%)
    all_gather x4, waiting for transfers between devices, spread(): value = lax.all_gather(value, axis).sum(axis=0)  139 us
    dot_general x16, matrix products, kernel_rows(): jnp.dot(centers, others.T, preferred_element_type=jnp.float32)  53.5 us
    all_to_all x4, blocking collectives, from_everyone(): return lax.all_to_all(copies, axis, split_axis=0, concat_axis=0, tiled=True)  41 us
    dot_general x1, matrix products, body(): jnp.einsum('nbs,bd->nsd', kernel, update_half, preferred_element_type=jnp...  19 us
    all_to_all x1, blocking collectives, summed_rows(): lax.all_to_all(nearer, far, split_axis=0, concat_axis=0, tiled=True)  18.2 us
    dot_general x1, matrix products, body(): jnp.einsum('nbs,nsd->bd', kernel, coef_tiles, preferred_element_type=jnp....  16.8 us
    reduce_sum x16, other arithmetic, kernel_rows(): point_squares = jnp.sum(other_wide * other_wide, axis=1)  16.8 us
    all_to_all x2, blocking collectives, sum_at_owner(): lax.all_to_all(pieces, axis, split_axis=0, concat_axis=0, tiled=True)  16.4 us
  transfers between devices with their start and end apart: 4, of which 4 were waited for; matrix products, arithmetic and copies ran while one was open for 0% of the time, Pallas kernels for 0%

profile of v1, /device:TPU:1, one launch (start us, length us, event | category | flops | bytes accessed | tf_op | source)
XLA Modules:
  0.0 370.1 jit_solution(4864867534452757038)
XLA Ops:
  7.2 1.6 copy.65
  9.5 2.0 dynamic-slice_select_fusion
  11.6 58.5 %all-gather.9.cloned.1.call-done = bf16[16384,128]{1,0:T(8,128)(2,1)} async-done(((bf16[2048,128]{1,0:T(8,128)(2,1)}), bf16[16384,128]{1,0:T(8,128)(2,1)}) %all-gather.9.cloned.1.call-update) | async-done | bytes 4194320 | tf_op jit(solution)/shard_map/all_gather | solution.py:15
  70.1 3.7 reduce_sum.93
  73.8 32.0 %all-gather.11.cloned.1.call-done = bf16[8192,128]{1,0:T(8,128)(2,1)} async-done(((bf16[2048,128]{1,0:T(8,128)(2,1)}), bf16[8192,128]{1,0:T(8,128)(2,1)}) %all-gather.11.cloned.1.call-update) | async-done | bytes 2097168 | tf_op jit(solution)/shard_map/all_gather | solution.py:15
  105.8 2.8 reduce_sum.94
  108.8 15.4 %all-gather.13.cloned.1.call-done = bf16[4096,128]{1,0:T(8,128)(2,1)} async-done(((bf16[2048,128]{1,0:T(8,128)(2,1)}), bf16[4096,128]{1,0:T(8,128)(2,1)}) %all-gather.13.cloned.1.call-update) | async-done | bytes 1048592 | tf_op jit(solution)/shard_map/all_gather | solution.py:15
  124.2 2.3 reduce_sum.95
  126.6 1.1 convert_element_type.26
  127.6 32.8 %all-gather.15.cloned.1.call-done = bf16[8192,128]{1,0:T(8,128)(2,1)} async-done(((bf16[2048,128]{1,0:T(8,128)(2,1)}), bf16[8192,128]{1,0:T(8,128)(2,1)}) %all-gather.15.cloned.1.call-update) | async-done | bytes 2097168 | tf_op jit(solution)/shard_map/all_gather | solution.py:15
  160.5 2.2 reduce_sum.96
  162.6 76.0 %while.10 = (s32[]{:T(128)}, bf16[16,2048,512]{1,2,0:T(8,128)(2,1)}, bf16[2048,128]{1,0:T(8,128)(2,1)S(1)}, bf16[16,512,128]{2,1,0:T(8,128)(2,1)}, s32[]{:T(128)}) while((s32[]{:T(128)}, bf16[16,2048,512]{1,2,0:T(8,128)(2,1)}, bf16[2048,128]{1,0:T(8,128)(2,1)S(1)}, bf16[16,512,128]{2,1,0:T(8,128)(2,1)}, s32[]{:T(128)}) %tuple.33), condition=%wide.region_7.8_spmd, body=%wide.region_4.7_spmd.sunk | while | flops 274658816 | bytes 3429441 | solution.py:95
  162.7 1.1 multiply_reduce_fusion.4
  163.7 0.3 multiply_reduce_fusion.5
  164.1 3.4 fusion.22
  167.4 1.0 multiply_reduce_fusion.4
  168.5 0.3 multiply_reduce_fusion.5
  168.8 3.3 fusion.22
  172.1 1.0 multiply_reduce_fusion.4
  173.5 3.3 fusion.22
  176.9 1.0 multiply_reduce_fusion.4
  178.3 3.4 fusion.22
  181.6 1.0 multiply_reduce_fusion.4
  183.0 3.4 fusion.22
  186.4 1.0 multiply_reduce_fusion.4
  187.8 3.3 fusion.22
  191.1 1.0 multiply_reduce_fusion.4
  192.5 3.4 fusion.22
  195.9 1.0 multiply_reduce_fusion.4
  197.3 3.3 fusion.22
  200.7 1.0 multiply_reduce_fusion.4
  202.1 3.4 fusion.22
  205.4 1.0 multiply_reduce_fusion.4
  206.8 3.3 fusion.22
  210.1 1.0 multiply_reduce_fusion.4
  211.5 3.3 fusion.22
  214.9 1.0 multiply_reduce_fusion.4
  216.3 3.4 fusion.22
  219.6 1.0 multiply_reduce_fusion.4
  220.7 0.3 multiply_reduce_fusion.5
  221.0 3.4 fusion.22
  224.4 1.0 multiply_reduce_fusion.4
  225.8 3.3 fusion.22
  229.1 1.0 multiply_reduce_fusion.4
  230.2 0.3 multiply_reduce_fusion.5
  230.5 3.4 fusion.22
  233.9 1.0 multiply_reduce_fusion.4
  235.3 3.3 fusion.22
  238.6 16.8 %fusion.8 = f32[2048,64]{0,1:T(8,128)S(1)} fusion(bf16[16,2048,512]{1,2,0:T(8,128)(2,1)} %get-tuple-element.24, bf16[8,16,8,512]{3,2,1,0:T(8,128)(2,1)} %bitcast.72, f32[8192,64]{0,1:T(8,128)} %param.9, s32[]{:T(128)S(6)} %select_n.44, f32[8192,64]{0,1:T(8,128)S(1)} %copy.65, pred[]{:T(512)S(6)} %eq.6), kind=kOutput, calls=%fused_computation.13 | convolution fusion | flops 2147876864 | bytes 36175876 | tf_op jit(solution)/shard_map/nbs,nsd->bd/dot_general | solution.py:96
  255.5 11.0 %all_to_all.35 = f32[4,512,64]{1,2,0:T(8,128)S(1)} all-to-all(f32[4,512,64]{1,2,0:T(8,128)S(1)} %bitcast.79), channel_id=1, replica_groups=mesh['pts_0'=8,'pts_1'=4,'pts_2'=2,'blk'=4] {'blk'}, dimensions={0} | all-to-all | bytes 1048576 | tf_op jit(solution)/shard_map/all_to_all | solution.py:26
  266.9 5.5 %all_to_all.36 = f32[2,1,16384]{2,1,0:T(1,128)S(1)} all-to-all(f32[2,1,16384]{2,1,0:T(1,128)S(1)} %reshape.36), channel_id=1, replica_groups=mesh['pts_0'=8,'pts_1'=4,'pts_2'=2,'blk'=4] {'pts_2'}, dimensions={0} | all-to-all | bytes 262144 | tf_op jit(solution)/shard_map/all_to_all | solution.py:26
  272.3 0.5 broadcast.16
  272.8 1.0 reduce.4
  274.2 18.2 %all_to_all.37 = f32[32,1,512]{2,1,0:T(1,128)S(1)} all-to-all(f32[32,1,512]{2,1,0:T(1,128)S(1)} %reshape.38), channel_id=1, replica_groups=mesh['pts_0'=8,'pts_1'=4,'pts_2'=2,'blk'=4] {'pts_0','pts_1'}, dimensions={0} | all-to-all | bytes 131072 | tf_op jit(solution)/shard_map/all_to_all | solution.py:34
  292.4 0.8 reduce.5
  293.5 12.0 %all_to_all.38 = f32[32,1,512]{2,1,0:T(1,128)S(1)} all-to-all(f32[32,1,512]{2,1,0:T(1,128)S(1)} %reshape.40), channel_id=1, replica_groups=mesh['pts_0'=8,'pts_1'=4,'pts_2'=2,'blk'=4] {'pts_0','pts_1'}, dimensions={0} | all-to-all | bytes 131072 | tf_op jit(solution)/shard_map/all_to_all | solution.py:45
  305.5 0.8 reduce.6
  306.6 6.6 %all_to_all.39 = f32[2,1,16384]{2,1,0:T(1,128)S(1)} all-to-all(f32[2,1,16384]{2,1,0:T(1,128)S(1)} %reshape.42), channel_id=1, replica_groups=mesh['pts_0'=8,'pts_1'=4,'pts_2'=2,'blk'=4] {'pts_2'}, dimensions={0} | all-to-all | bytes 262144 | tf_op jit(solution)/shard_map/all_to_all | solution.py:45
  313.2 1.0 reduce.7
  314.6 11.6 %all_to_all.40 = f32[4,512,64]{1,2,0:T(8,128)S(1)} all-to-all(f32[4,512,64]{1,2,0:T(8,128)S(1)} %broadcast_in_dim.33), channel_id=1, replica_groups=mesh['pts_0'=8,'pts_1'=4,'pts_2'=2,'blk'=4] {'blk'}, dimensions={0} | all-to-all | bytes 1048576 | tf_op jit(solution)/shard_map/all_to_all | solution.py:45
  326.2 6.3 %convolution_bitcast_fusion.1 = f32[512,64]{0,1:T(8,128)S(1)} fusion(f32[2048,64]{0,1:T(8,128)S(1)} %bitcast.76, f32[512,2048]{1,0:T(8,128)} %param.12), kind=kOutput, calls=%fused_computation.14 | convolution fusion | flops 805306368 | bytes 4849664 | tf_op jit(solution)/shard_map/dot_general | solution.py:103
  332.6 10.8 %all_to_all.41 = f32[4,512,64]{1,2,0:T(8,128)S(1)} all-to-all(f32[4,512,64]{1,2,0:T(8,128)S(1)} %broadcast_in_dim.34), channel_id=1, replica_groups=mesh['pts_0'=8,'pts_1'=4,'pts_2'=2,'blk'=4] {'blk'}, dimensions={0} | all-to-all | bytes 1048576 | tf_op jit(solution)/shard_map/all_to_all | solution.py:45
  343.7 0.8 select_n.49
  344.5 19.0 %convolution_add_fusion = f32[8192,64]{0,1:T(8,128)} fusion(f32[8192,64]{0,1:T(8,128)} %param.11, bf16[8192,2048]{1,0:T(8,128)(2,1)} %bitcast.71, bf16[2048,64]{0,1:T(8,128)(2,1)S(1)} %bitcast.82), kind=kOutput, calls=%fused_computation.11 | convolution fusion | flops 2148007936 | bytes 38010880 | tf_op jit(solution)/shard_map/nbs,bd->nsd/dot_general | solution.py:109
  (48 shorter events, 6.4 us)
Async XLA Ops:
  7.2 62.9 %all-gather.9.cloned.1.call-start = ((), (), s32[]{:S(2)}) async-start(), calls=%async_computation.7 | async-start | bytes 4718592 | tf_op jit(solution)/shard_map/all_gather | solution.py:15
  11.5 94.3 %all-gather.11.cloned.1.call-start = ((), (), s32[]{:S(2)}) async-start(), calls=%async_computation.8 | async-start | bytes 2621440 | tf_op jit(solution)/shard_map/all_gather | solution.py:15
  73.8 50.4 %all-gather.13.cloned.1.call-start = ((), (), s32[]{:S(2)}) async-start(), calls=%async_computation.9 | async-start | bytes 1572864 | tf_op jit(solution)/shard_map/all_gather | solution.py:15
  108.7 51.8 %all-gather.15.cloned.1.call-start = ((), (), s32[]{:S(2)}) async-start(), calls=%async_computation.10 | async-start | bytes 2621440 | tf_op jit(solution)/shard_map/all_gather | solution.py:15
  344.5 19.1 %copy-start = (f32[8192,64]{0,1:T(8,128)}, f32[8192,64]{0,1:T(8,128)S(1)}, u32[]{:S(2)}) copy-start(f32[8192,64]{0,1:T(8,128)S(1)} %select_n.49) | copy-start | bytes 6291460
Sparse Core Ops, SparseCore 0:
  11.7 58.3 all-gather.8
  73.9 31.8 all-gather.10
  108.8 15.3 all-gather.12
  126.7 33.7 all-gather.14
